TPU v7x, 512 devices: a whole 4x8x8 slice. The times are simulated.
512 devices in a mesh: ta: 8 (over z), af: 8 (over y_lo, x), sa: 8 (over y_hi, core).
Axes of the slice: x: 4, y: 8 (y_hi: 4, y_lo: 2; y = y_hi * 2 + y_lo), z: 8, core: 2. Of those that a mesh axis runs over, the one named last changes fastest.
Arguments:
- blocks: bfloat16 [8, 8, 8, 4, 64, 4096], P('ta', 'af', 'sa'), may hold values from -6 to 6
- coords: int32 [8, 8, 8, 4, 3], P('ta', 'af', 'sa'), may hold values from 0 to 1, as said below
- counts: int32 [8, 8, 8], P('ta', 'af', 'sa'), may hold values from 1 to 4, as said below
- time_factor: float32 [8, 128, 256], P('ta', ('af', 'sa')), may hold values from -2.4 to 2.4
- freq_factor: float32 [8, 128, 256], P('af', ('ta', 'sa')), may hold values from -2.4 to 2.4
- subj_factor: float32 [8, 128, 256], P('sa', ('ta', 'af')), may hold values from -2.4 to 2.4
- time_velocity: float32 [8, 128, 256], P('ta', ('af', 'sa')), may hold values from -1.8 to 1.8
- freq_velocity: float32 [8, 128, 256], P('af', ('ta', 'sa')), may hold values from -1.8 to 1.8
- subj_velocity: float32 [8, 128, 256], P('sa', ('ta', 'af')), may hold values from -1.8 to 1.8
Outputs:
- new_time: float32 [8, 128, 256], P('ta', ('af', 'sa'))
- new_freq: float32 [8, 128, 256], P('af', ('ta', 'sa'))
- new_subj: float32 [8, 128, 256], P('sa', ('ta', 'af'))
- new_time_velocity: float32 [8, 128, 256], P('ta', ('af', 'sa'))
- new_freq_velocity: float32 [8, 128, 256], P('af', ('ta', 'sa'))
- new_subj_velocity: float32 [8, 128, 256], P('sa', ('ta', 'af'))
Inputs may be any that keep to these rules, and one draw needn't show every extreme that they name: `coords`: entries are 0 or 1; the 4 slots of a device name distinct positions. `counts`: some device has 4 filled slots and some has 1.
All inputs are finite; a program needn't handle non-finite values.
Results may differ from a plain program's by a relative error of at most 0.005.
Values may be sent and summed in bfloat16 or wider, within the bound.
No kernel may reach another device: no remote copies, remote signals or barrier semaphores. Data moves between devices by JAX's collectives and lax.ppermute only.
A program may use at most 64 MiB of HBM per device.

v0:
```python
import jax
import jax.numpy as jnp
from jax import lax
from jax.sharding import PartitionSpec as P

BF = 64
BS = 64


def block_terms(
    block_data, time_table, freq_table, subj_table, position, valid, freq_extent, subj_extent
):
    time_extent = block_data.shape[0]
    time_block = lax.dynamic_slice_in_dim(time_table, position[0] * time_extent, time_extent, 0)
    freq_block = lax.dynamic_slice_in_dim(freq_table, position[1] * freq_extent, freq_extent, 0)
    subj_block = lax.dynamic_slice_in_dim(subj_table, position[2] * subj_extent, subj_extent, 0)
    freq_wide = freq_block.astype(jnp.float32)
    subj_wide = subj_block.astype(jnp.float32)
    khatri = (freq_wide[:, None, :] * subj_wide[None, :, :]).astype(jnp.bfloat16)
    khatri = khatri.reshape(freq_extent * subj_extent, -1)
    approx = lax.dot_general(
        time_block, khatri, (((1,), (1,)), ((), ())), preferred_element_type=jnp.float32
    )
    observed = block_data.astype(jnp.float32)
    misfit = ((approx - observed) * valid).astype(jnp.bfloat16)
    grad_time = jnp.dot(misfit, khatri, preferred_element_type=jnp.float32)
    contracted = lax.dot_general(
        misfit, time_block, (((0,), (0,)), ((), ())), preferred_element_type=jnp.float32
    )
    contracted = contracted.reshape(freq_extent, subj_extent, -1)
    grad_freq = jnp.sum(contracted * subj_wide[None, :, :], axis=1)
    grad_subj = jnp.sum(contracted * freq_wide[:, None, :], axis=0)
    return (grad_time, grad_freq, grad_subj)


def add_rows(accumulated, block_grad, offset):
    current = lax.dynamic_slice_in_dim(accumulated, offset, block_grad.shape[0], 0)
    return lax.dynamic_update_slice_in_dim(accumulated, current + block_grad, offset, 0)


def per_device(
    blocks,
    coords,
    counts,
    time_factor,
    freq_factor,
    subj_factor,
    time_velocity,
    freq_velocity,
    subj_velocity,
):
    time_table = lax.all_gather(time_factor.astype(jnp.bfloat16), ("af", "sa"), axis=1, tiled=True)[
        0
    ]
    freq_table = lax.all_gather(freq_factor.astype(jnp.bfloat16), ("ta", "sa"), axis=1, tiled=True)[
        0
    ]
    subj_table = lax.all_gather(subj_factor.astype(jnp.bfloat16), ("ta", "af"), axis=1, tiled=True)[
        0
    ]
    local_blocks = blocks[0, 0, 0]
    local_coords = coords[0, 0, 0]
    filled = counts[0, 0, 0]
    time_extent = local_blocks.shape[1]
    freq_extent = BF
    subj_extent = BS

    def visit_slot(slot_index, running, valid):
        position = local_coords[slot_index]
        grad_time, grad_freq, grad_subj = block_terms(
            local_blocks[slot_index],
            time_table,
            freq_table,
            subj_table,
            position,
            valid,
            freq_extent,
            subj_extent,
        )
        return (
            add_rows(running[0], grad_time, position[0] * time_extent),
            add_rows(running[1], grad_freq, position[1] * freq_extent),
            add_rows(running[2], grad_subj, position[2] * subj_extent),
        )

    initial = (
        jnp.zeros(time_table.shape, jnp.float32),
        jnp.zeros(freq_table.shape, jnp.float32),
        jnp.zeros(subj_table.shape, jnp.float32),
    )
    running = lax.fori_loop(
        0,
        local_blocks.shape[0],
        lambda slot_index, running: visit_slot(
            slot_index, running, (slot_index < filled).astype(jnp.float32)
        ),
        initial,
    )
    time_grad = lax.psum_scatter(running[0][None], ("af", "sa"), scatter_dimension=1, tiled=True)
    freq_grad = lax.psum_scatter(running[1][None], ("ta", "sa"), scatter_dimension=1, tiled=True)
    subj_grad = lax.psum_scatter(running[2][None], ("ta", "af"), scatter_dimension=1, tiled=True)
    new_time_velocity = 0.9 * time_velocity + time_grad / 64.0
    new_freq_velocity = 0.9 * freq_velocity + freq_grad / 64.0
    new_subj_velocity = 0.9 * subj_velocity + subj_grad / 64.0
    new_time = time_factor - 0.5 * new_time_velocity
    new_freq = freq_factor - 0.5 * new_freq_velocity
    new_subj = subj_factor - 0.5 * new_subj_velocity
    return (new_time, new_freq, new_subj, new_time_velocity, new_freq_velocity, new_subj_velocity)


def solution(mesh):
    return jax.shard_map(
        per_device,
        mesh=mesh,
        in_specs=(
            P("ta", "af", "sa", None, None, None),
            P("ta", "af", "sa", None, None),
            P("ta", "af", "sa"),
            P("ta", ("af", "sa"), None),
            P("af", ("ta", "sa"), None),
            P("sa", ("ta", "af"), None),
            P("ta", ("af", "sa"), None),
            P("af", ("ta", "sa"), None),
            P("sa", ("ta", "af"), None),
        ),
        out_specs=(
            P("ta", ("af", "sa"), None),
            P("af", ("ta", "sa"), None),
            P("sa", ("ta", "af"), None),
            P("ta", ("af", "sa"), None),
            P("af", ("ta", "sa"), None),
            P("sa", ("ta", "af"), None),
        ),
        check_vma=False,
    )
```

profile of v0, /device:TPU:2, one launch (start us, length us, event | category | flops | bytes accessed | tf_op | source)
XLA Modules:
  0.0 1572.2 jit_solution(18307715518159447462)
XLA Ops:
  7.2 0.8 copy.20
  8.0 0.7 copy.41
  8.7 71.2 %all_gather.9 = bf16[1,128,256]{2,0,1:T(2,128)(2,1)S(1)} all-gather(bf16[1,2,256]{2,0,1:T(2,128)(2,1)S(1)} %copy.41), channel_id=1, replica_groups=mesh['ta'=8,'af'=8,'sa'=8] {'af','sa'}, dimensions={1}, use_global_device_ids=true | all-gather | bytes 66560 | tf_op jit(solution)/shard_map/all_gather | solution.py:52
  79.9 0.7 copy.40
  80.6 88.1 %all_gather.10 = bf16[1,128,256]{2,0,1:T(2,128)(2,1)S(1)} all-gather(bf16[1,2,256]{2,0,1:T(2,128)(2,1)S(1)} %copy.40), channel_id=1, replica_groups=mesh['ta'=8,'af'=8,'sa'=8] {'ta','sa'}, dimensions={1}, use_global_device_ids=true | all-gather | bytes 66560 | tf_op jit(solution)/shard_map/all_gather | solution.py:55
  168.7 0.7 copy.39
  169.4 155.6 %all_gather.11 = bf16[1,128,256]{2,0,1:T(2,128)(2,1)S(1)} all-gather(bf16[1,2,256]{2,0,1:T(2,128)(2,1)S(1)} %copy.39), channel_id=1, replica_groups=mesh['ta'=8,'af'=8,'sa'=8] {'ta','af'}, dimensions={1}, use_global_device_ids=true | all-gather | bytes 66560 | tf_op jit(solution)/shard_map/all_gather | solution.py:58
  325.1 30.4 %while.17 = (s32[]{:T(128)}, f32[128,256]{1,0:T(8,128)S(1)}, f32[128,256]{1,0:T(8,128)S(1)}, f32[128,256]{1,0:T(8,128)S(1)}, s32[4,3]{1,0:T(4,128)S(1)}, /*index...) while((s32[]{:T(128)}, f32[128,256]{1,0:T(8,128)S(1)}, ...), condition=%wide.region_3.0_spmd, body=%wide.region_0.0_spmd.sunk | while | flops 410042368 | bytes 17957244 | solution.py:91
  327.7 0.7 multiply_convert_fusion.2
  329.1 1.8 fusion.33
  331.3 0.8 multiply_reduce_fusion.4
  335.3 0.7 multiply_convert_fusion.2
  336.7 1.8 fusion.33
  338.9 0.8 multiply_reduce_fusion.4
  342.9 0.7 multiply_convert_fusion.2
  344.3 1.8 fusion.33
  346.5 0.8 multiply_reduce_fusion.4
  350.5 0.7 multiply_convert_fusion.2
  351.9 1.8 fusion.33
  354.2 0.8 multiply_reduce_fusion.4
  355.5 0.6 copy-done
  356.2 0.7 all-reduce.9.cloned.1.call-update
  357.0 0.7 all-reduce.11.cloned.1.call-update
  357.7 1.3 dynamic-slice
  358.9 1.3 dynamic-slice.2
  361.5 1.3 dynamic-slice.4
  363.4 171.6 %all-reduce.7.cloned.1.call-done = f32[1,128,256]{2,1,0:T(8,128)} async-done(((f32[1,128,256]{2,1,0:T(8,128)}), f32[1,128,256]{2,1,0:T(8,128)}) %all-reduce.7.cloned.1.call-update) | async-done | bytes 131088
  535.0 1.3 multiply_subtract_fusion.2
  536.3 490.8 %all-reduce.9.cloned.1.call-done = f32[1,128,256]{2,1,0:T(8,128)} async-done(((f32[1,128,256]{2,1,0:T(8,128)}), f32[1,128,256]{2,1,0:T(8,128)}) %all-reduce.9.cloned.1.call-update) | async-done | bytes 131088
  1027.1 1.3 multiply_subtract_fusion.1
  1028.4 535.9 %all-reduce.11.cloned.1.call-done = f32[1,128,256]{2,1,0:T(8,128)} async-done(((f32[1,128,256]{2,1,0:T(8,128)}), f32[1,128,256]{2,1,0:T(8,128)}) %all-reduce.11.cloned.1.call-update) | async-done | bytes 131088
  1564.4 1.3 multiply_subtract_fusion
  (55 shorter events, 6.9 us)
Async XLA Ops:
  7.2 527.8 %all-reduce.7.cloned.1.call-start = ((), (), s32[]{:S(2)}) async-start(), calls=%async_computation | async-start | bytes 262144
  325.0 210.0 %copy-start.3 = (f32[1,2,256]{2,1,0:T(2,128)S(1)}, f32[1,2,256]{2,1,0:T(2,128)}, u32[]{:S(2)}) copy-start(f32[1,2,256]{2,1,0:T(2,128)} %param.14) | copy-start | bytes 6148
  325.0 210.0 %copy-start.6 = (f32[1,2,256]{2,1,0:T(2,128)S(1)}, f32[1,2,256]{2,1,0:T(2,128)}, u32[]{:S(2)}) copy-start(f32[1,2,256]{2,1,0:T(2,128)} %param.17) | copy-start | bytes 6148
  325.0 702.1 %copy-start.4 = (f32[1,2,256]{2,1,0:T(2,128)S(1)}, f32[1,2,256]{2,1,0:T(2,128)}, u32[]{:S(2)}) copy-start(f32[1,2,256]{2,1,0:T(2,128)} %param.15) | copy-start | bytes 6148
  325.0 702.1 %copy-start.7 = (f32[1,2,256]{2,1,0:T(2,128)S(1)}, f32[1,2,256]{2,1,0:T(2,128)}, u32[]{:S(2)}) copy-start(f32[1,2,256]{2,1,0:T(2,128)} %param.18) | copy-start | bytes 6148
  325.1 1239.3 %copy-start.5 = (f32[1,2,256]{2,1,0:T(2,128)S(1)}, f32[1,2,256]{2,1,0:T(2,128)}, u32[]{:S(2)}) copy-start(f32[1,2,256]{2,1,0:T(2,128)} %param.16) | copy-start | bytes 6148
  325.1 1239.3 %copy-start.8 = (f32[1,2,256]{2,1,0:T(2,128)S(1)}, f32[1,2,256]{2,1,0:T(2,128)}, u32[]{:S(2)}) copy-start(f32[1,2,256]{2,1,0:T(2,128)} %param.19) | copy-start | bytes 6148
  355.5 0.6 copy-start
  355.5 0.7 copy-start.1
  355.5 1.5 copy-start.2
  356.2 671.0 %all-reduce.9.cloned.1.call-start = ((), (), s32[]{:S(2)}) async-start(), calls=%async_computation.1 | async-start | bytes 262144
  356.9 1207.4 %all-reduce.11.cloned.1.call-start = ((), (), s32[]{:S(2)}) async-start(), calls=%async_computation.2 | async-start | bytes 262144
Sparse Core Ops, SparseCore 0:
  356.3 178.6 all-reduce.6
  537.9 489.1 all-reduce.8
  1030.3 534.0 all-reduce.10
where the time goes:
time: 1570 us
  waiting for transfers between devices  1200 us (76%)
  blocking collectives  315 us (20%)
  between operations  15.8 us (1%)
    unnamed x6, waiting for transfers between devices  1200 us
    all_gather x1, blocking collectives, per_device(): lax.all_gather(subj_factor.astype(jnp.bfloat16), ('ta', 'af'), axis=1, ti...  156 us
    all_gather x1, blocking collectives, per_device(): lax.all_gather(freq_factor.astype(jnp.bfloat16), ('ta', 'sa'), axis=1, ti...  88.1 us
    all_gather x1, blocking collectives, per_device(): lax.all_gather(time_factor.astype(jnp.bfloat16), ('af', 'sa'), axis=1, ti...  71.2 us
  transfers between devices with their start and end apart: 3, of which 3 were waited for; matrix products, arithmetic and copies ran while one was open for 0% of the time, Pallas kernels for 0%

commit v1 on v0

--- a/solution.py
+++ b/solution.py
@@ -52,9 +52,15 @@
     time_table = lax.all_gather(time_factor.astype(jnp.bfloat16), ("af", "sa"), axis=1, tiled=True)[
         0
     ]
-    freq_table = lax.all_gather(freq_factor.astype(jnp.bfloat16), ("ta", "sa"), axis=1, tiled=True)[
-        0
-    ]
+    freq_table = jnp.concatenate(
+        lax.all_to_all(
+            jnp.stack([freq_factor.astype(jnp.bfloat16)] * lax.axis_size(("ta", "sa"))),
+            ("ta", "sa"),
+            0,
+            0,
+        ),
+        axis=1,
+    )[0]
     subj_table = lax.all_gather(subj_factor.astype(jnp.bfloat16), ("ta", "af"), axis=1, tiled=True)[
         0
     ]

time: 1570 us -> 1510 us (0.962)
  blocking collectives: 315 us -> 236 us
  starting transfers between devices: 0.12 us -> 16.7 us
    all_gather x1 -> x0, blocking collectives: 88.1 us -> none  [per_device(): lax.all_gather(freq_factor.astype(jnp.bfloat16), ('ta', 'sa'), axis=1, ti...]
    all_to_all x0 -> x1, starting transfers between devices: none -> 16.6 us  [per_device(): lax.all_to_all(jnp.stack([freq_factor.astype(jnp.bfloat16)] * lax.axis_si...]
  transfers between devices with their start and end apart: 3 -> 4, of which waited for: 3 -> 3; matrix products, arithmetic and copies ran while one was open for 0% -> 1% of each run, Pallas kernels for 0% -> 0%
where the time goes in v1:
time: 1510 us
  waiting for transfers between devices  1200 us (79%)
  blocking collectives  236 us (16%)
  starting transfers between devices  16.7 us (1%)
  between operations  15.9 us (1%)
    unnamed x6, waiting for transfers between devices  1200 us
    all_gather x1, blocking collectives, per_device(): lax.all_gather(subj_factor.astype(jnp.bfloat16), ('ta', 'af'), axis=1, ti...  165 us
    all_gather x1, blocking collectives, per_device(): lax.all_gather(time_factor.astype(jnp.bfloat16), ('af', 'sa'), axis=1, ti...  70.7 us
  transfers between devices with their start and end apart: 4, of which 3 were waited for; matrix products, arithmetic and copies ran while one was open for 1% of the time, Pallas kernels for 0%

profile of v1, /device:TPU:2, one launch (start us, length us, event | category | flops | bytes accessed | tf_op | source)
XLA Modules:
  0.0 1507.4 jit_solution(16958666439071936763)
XLA Ops:
  7.2 0.7 convert_bitcast_fusion
  8.5 16.6 %all-to-all-start = ((bf16[64,1,2,256]{3,2,1,0:T(2,128)(2,1)}), bf16[64,1,2,256]{3,2,1,0:T(2,128)(2,1)S(1)}, u32[]{:S(2)}, u32[]{:S(2)}) async-start(bf16[64,1,2,256]{3,2,1,0:T(2,128)(2,1)} %stack.2), calls=%async_computation | async-start | bytes 131072 | tf_op jit(solution)/shard_map/all_to_all | solution.py:56
  25.2 0.8 copy.19
  25.9 0.7 copy.35
  26.6 70.7 %all_gather.6 = bf16[1,128,256]{2,0,1:T(2,128)(2,1)S(1)} all-gather(bf16[1,2,256]{2,0,1:T(2,128)(2,1)S(1)} %copy.35), channel_id=1, replica_groups=mesh['ta'=8,'af'=8,'sa'=8] {'af','sa'}, dimensions={1}, use_global_device_ids=true | all-gather | bytes 66560 | tf_op jit(solution)/shard_map/all_gather | solution.py:52
  97.3 0.7 copy.34
  98.0 165.3 %all_gather.7 = bf16[1,128,256]{2,0,1:T(2,128)(2,1)S(1)} all-gather(bf16[1,2,256]{2,0,1:T(2,128)(2,1)S(1)} %copy.34), channel_id=1, replica_groups=mesh['ta'=8,'af'=8,'sa'=8] {'ta','af'}, dimensions={1}, use_global_device_ids=true | all-gather | bytes 66560 | tf_op jit(solution)/shard_map/all_gather | solution.py:64
  263.5 30.9 %while.17 = (s32[]{:T(128)}, f32[128,256]{1,0:T(8,128)S(1)}, f32[128,256]{1,0:T(8,128)S(1)}, f32[128,256]{1,0:T(8,128)S(1)}, s32[4,3]{1,0:T(4,128)S(1)}, /*index...) while((s32[]{:T(128)}, f32[128,256]{1,0:T(8,128)S(1)}, ...), condition=%wide.region_3.0_spmd, body=%wide.region_0.0_spmd.sunk | while | flops 410042368 | bytes 17957244 | solution.py:97
  266.1 0.7 multiply_convert_fusion.2
  267.4 1.8 fusion.33
  269.7 0.8 multiply_reduce_fusion.4
  270.5 0.7 multiply_reduce_fusion.5
  273.8 0.7 multiply_convert_fusion.2
  275.2 1.8 fusion.33
  277.4 0.8 multiply_reduce_fusion.4
  278.2 0.7 multiply_reduce_fusion.5
  281.5 0.7 multiply_convert_fusion.2
  282.9 1.8 fusion.33
  285.2 0.8 multiply_reduce_fusion.4
  289.3 0.7 multiply_convert_fusion.2
  290.6 1.8 fusion.33
  292.9 0.8 multiply_reduce_fusion.4
  295.1 0.7 all-reduce.9.cloned.1.call-update
  295.8 1.3 dynamic-slice
  297.1 1.3 dynamic-slice.2
  299.7 1.3 dynamic-slice.4
  301.6 168.6 %all-reduce.7.cloned.1.call-done = f32[1,128,256]{2,1,0:T(8,128)} async-done(((f32[1,128,256]{2,1,0:T(8,128)}), f32[1,128,256]{2,1,0:T(8,128)}) %all-reduce.7.cloned.1.call-update) | async-done | bytes 131088
  470.2 1.3 multiply_subtract_fusion.2
  471.5 490.8 %all-reduce.9.cloned.1.call-done = f32[1,128,256]{2,1,0:T(8,128)} async-done(((f32[1,128,256]{2,1,0:T(8,128)}), f32[1,128,256]{2,1,0:T(8,128)}) %all-reduce.9.cloned.1.call-update) | async-done | bytes 131088
  962.4 1.3 multiply_subtract_fusion.1
  963.6 535.9 %all-reduce.11.cloned.1.call-done = f32[1,128,256]{2,1,0:T(8,128)} async-done(((f32[1,128,256]{2,1,0:T(8,128)}), f32[1,128,256]{2,1,0:T(8,128)}) %all-reduce.11.cloned.1.call-update) | async-done | bytes 131088
  1499.6 1.3 multiply_subtract_fusion
  (57 shorter events, 7.4 us)
Async XLA Ops:
  8.5 254.8 %all-to-all-start = ((bf16[64,1,2,256]{3,2,1,0:T(2,128)(2,1)}), bf16[64,1,2,256]{3,2,1,0:T(2,128)(2,1)S(1)}, u32[]{:S(2)}, u32[]{:S(2)}) async-start(bf16[64,1,2,256]{3,2,1,0:T(2,128)(2,1)} %stack.2), calls=%async_computation | async-start | bytes 131072 | tf_op jit(solution)/shard_map/all_to_all | solution.py:56
  25.1 445.1 %all-reduce.7.cloned.1.call-start = ((), (), s32[]{:S(2)}) async-start(), calls=%async_computation.1 | async-start | bytes 262144
  263.4 206.8 %copy-start.3 = (f32[1,2,256]{2,1,0:T(2,128)S(1)}, f32[1,2,256]{2,1,0:T(2,128)}, u32[]{:S(2)}) copy-start(f32[1,2,256]{2,1,0:T(2,128)} %param.14) | copy-start | bytes 6148
  263.4 206.8 %copy-start.6 = (f32[1,2,256]{2,1,0:T(2,128)S(1)}, f32[1,2,256]{2,1,0:T(2,128)}, u32[]{:S(2)}) copy-start(f32[1,2,256]{2,1,0:T(2,128)} %param.17) | copy-start | bytes 6148
  263.4 698.9 %copy-start.4 = (f32[1,2,256]{2,1,0:T(2,128)S(1)}, f32[1,2,256]{2,1,0:T(2,128)}, u32[]{:S(2)}) copy-start(f32[1,2,256]{2,1,0:T(2,128)} %param.15) | copy-start | bytes 6148
  263.4 698.9 %copy-start.7 = (f32[1,2,256]{2,1,0:T(2,128)S(1)}, f32[1,2,256]{2,1,0:T(2,128)}, u32[]{:S(2)}) copy-start(f32[1,2,256]{2,1,0:T(2,128)} %param.18) | copy-start | bytes 6148
  263.4 1236.1 %copy-start.5 = (f32[1,2,256]{2,1,0:T(2,128)S(1)}, f32[1,2,256]{2,1,0:T(2,128)}, u32[]{:S(2)}) copy-start(f32[1,2,256]{2,1,0:T(2,128)} %param.16) | copy-start | bytes 6148
  263.5 1236.1 %copy-start.8 = (f32[1,2,256]{2,1,0:T(2,128)S(1)}, f32[1,2,256]{2,1,0:T(2,128)}, u32[]{:S(2)}) copy-start(f32[1,2,256]{2,1,0:T(2,128)} %param.19) | copy-start | bytes 6148
  294.4 0.6 copy-start
  294.4 0.7 copy-start.1
  294.4 7.2 copy-start.2
  295.0 667.3 %all-reduce.9.cloned.1.call-start = ((), (), s32[]{:S(2)}) async-start(), calls=%async_computation.2 | async-start | bytes 262144
  295.8 1203.8 %all-reduce.11.cloned.1.call-start = ((), (), s32[]{:S(2)}) async-start(), calls=%async_computation.3 | async-start | bytes 262144
Sparse Core Ops, SparseCore 0:
  295.2 175.0 all-reduce.6
  473.1 489.1 all-reduce.8
  965.5 534.0 all-reduce.10
